TPU v7x, 256 devices: a whole 4x4x8 slice. The times are simulated.
256 devices in a mesh: space: 64 (over z, x, core), inst: 4 (over y).
Axes of the slice: x: 4, y: 4, z: 8, core: 2. Of those that a mesh axis runs over, the one named last changes fastest.
Arguments:
- adjoint: float32 [8, 5, 131072], P('inst', None, 'space'), may hold values from -6 to 6
- jac_cell: float32 [8, 5, 5, 131072], P('inst', None, None, 'space'), may hold values from -2.5 to 2.5
- jac_left: float32 [8, 5, 5, 131072], P('inst', None, None, 'space'), may hold values from -2.5 to 2.5
- jac_right: float32 [8, 5, 5, 131072], P('inst', None, None, 'space'), may hold values from -2.5 to 2.5
- volume: float32 [131072], P('space'), may hold values from 0.5 to 2
- normals: float32 [3, 131072], P(None, 'space'), may hold values from -6 to 6
- surface: int32 [131072], P('space'), may hold values 0 or 1
- instance_map: int32 [8], replicated, may hold values from 0 to 7, each once
- mode_shapes: float32 [200, 3, 131072], P(None, None, 'space'), may hold values from -0.01953125 to 0.01953125
- damping: float32 [200], replicated, may hold values from 0.2 to 2
- modal_inverse: float32 [200, 200], replicated, may hold values from -2 to 3
Outputs:
- flow_residual: float32 [8, 5, 131072], P('inst', None, 'space')
- mesh_forcing: float32 [8, 3, 131072], P('inst', None, 'space')
- modal_adjoint: float32 [8, 200], P('inst')
All inputs are finite; a program needn't handle non-finite values. No bound on the sum of `surface` on one device may be relied on, other than what follows from the above.
Results may differ from a plain program's by a relative error of at most 0.000068.
Values sent between devices are 32-bit elements; how exact they have to be, the bound alone decides.
A program may use at most 64 MiB of HBM per device.

v0:
```python
import jax
import jax.numpy as jnp
from jax import lax
from jax.sharding import PartitionSpec as P


def padded_2(shard, sides, width):
    for axis, dim in sides:
        count, length = (lax.axis_size(axis), shard.shape[dim])
        up = [(i, (i + 1) % count) for i in range(count - 1)]
        down = [(j, i) for i, j in up]
        last = lax.slice_in_dim(shard, length - width, length, axis=dim)
        leading = lax.slice_in_dim(shard, 0, width, axis=dim)
        before = lax.ppermute(last, axis, up)
        after = lax.ppermute(leading, axis, down)
        shard = jnp.concatenate([before, shard, after], axis=dim)
    return shard


def coupling_matrix(instance_map):
    count = instance_map.shape[0]
    slots = instance_map.astype(jnp.float32)
    differ = slots[:, None] - slots[None, :]
    angle = jnp.pi * differ / count
    same = differ == 0
    sine = jnp.where(same, 1.0, jnp.sin(angle))
    return jnp.where(same, 0.0, 0.5 * jnp.cos(jnp.pi * differ) * jnp.cos(angle) / sine)


def shards(
    adjoint,
    jac_cell,
    jac_left,
    jac_right,
    volume,
    normals,
    surface,
    instance_map,
    mode_shapes,
    damping,
    modal_inverse,
):
    highest = lax.Precision.HIGHEST
    own_slots = adjoint.shape[0]
    modes = mode_shapes.shape[0]
    first_slot = lax.axis_index("inst") * own_slots
    coupling = coupling_matrix(instance_map)
    own_cols = lax.dynamic_slice_in_dim(coupling, first_slot, own_slots, 1)
    flow = jnp.einsum("sfec,sfc->sec", jac_cell, adjoint, precision=highest)
    from_left = jnp.einsum("sfec,sfc->sec", jac_left, adjoint, precision=highest)
    from_right = jnp.einsum("sfec,sfc->sec", jac_right, adjoint, precision=highest)
    stacked = jnp.stack([from_left, from_right])
    padded = padded_2(stacked, (("space", 3),), 1)
    flow = flow + padded[0, :, :, 2:] + padded[1, :, :, :-2]
    timed = jnp.einsum(
        "ab,aec->bec",
        own_cols,
        lax.all_gather(adjoint, "inst", axis=0, tiled=True),
        precision=highest,
    )
    flow = flow + volume[None, None, :] * timed
    walls = surface.astype(jnp.float32)
    force = (walls[None, :] * flow[:, 4, :])[:, None, :] * normals[None, :, :]
    shapes = mode_shapes.reshape(modes, -1)
    projected = lax.dot_general(
        force.reshape(own_slots, -1),
        shapes,
        (((1,), (1,)), ((), ())),
        precision=highest,
        preferred_element_type=jnp.float32,
    )
    summed = lax.psum(projected, "space")
    gathered = lax.all_gather(summed, "inst", axis=0, tiled=True)
    own_projected = lax.dynamic_slice_in_dim(gathered, first_slot, own_slots, 0)
    modal_rhs = own_projected + damping[None, :] * jnp.dot(own_cols.T, gathered, precision=highest)
    modal_adjoint = jnp.dot(modal_rhs, modal_inverse, precision=highest)
    expanded = jnp.dot(modal_adjoint, shapes, precision=highest).reshape(own_slots, 3, -1)
    mesh_forcing = walls[None, None, :] * expanded
    return (flow, mesh_forcing, modal_adjoint)


def solution(mesh):
    placed = (
        P("inst", None, "space"),
        P("inst", None, None, "space"),
        P("inst", None, None, "space"),
        P("inst", None, None, "space"),
        P("space"),
        P(None, "space"),
        P("space"),
        P(),
        P(None, None, "space"),
        P(),
        P(),
    )
    return jax.shard_map(
        shards,
        mesh=mesh,
        in_specs=placed,
        out_specs=(P("inst", None, "space"), P("inst", None, "space"), P("inst", None)),
        check_vma=False,
    )
```

profile of v0, /device:TPU:8, one launch (start us, length us, event | category | flops | bytes accessed | tf_op | source)
XLA Modules:
  0.0 175.6 jit_solution(5606615448060914393)
XLA Ops:
  0.6 0.0 copy-start
  0.6 0.0 copy-start.3
  0.7 2.1 %multiply_reduce_fusion.2 = (f32[2,2048,5]{1,0,2:T(2,128)S(1)}, f32[2,2048,5]{1,0,2:T(2,128)S(1)}, f32[2,2048,5]{1,0,2:T(2,128)S(1)}) fusion(f32[2,5,5,2048]{3,0,2,1:T(2,128)} %param.12, f32[2,2048,5]{1,0,2:T(2,128)} %bitcast.61, f32[2,5,5,2048]{3,0,2,1:T(2,128)} %param.13, f32[2,5,5,2048]{3,0,2,1:T(2,128)} %param.14), kind=kLoop, calls=%fused_computation.10 | loop fusion | flops 552960 | bytes 1556480 | tf_op jit(solution)/shard_map/sfec,sfc->sec/dot_general | solution.py:49
  2.8 0.1 pad_maximum_fusion.5
  2.9 1.7 collective-permute-start.1
  4.6 1.3 collective-permute-start
  5.9 0.9 copy.16
  6.8 13.6 %all_gather.6 = f32[8,5,2048]{2,1,0:T(8,128)S(1)} all-gather(f32[2,5,2048]{2,1,0:T(8,128)S(1)} %copy.16), channel_id=1, replica_groups=mesh['space'=64,'inst'=4] {'inst'}, dimensions={0}, use_global_device_ids=true | all-gather | bytes 409600 | tf_op jit(solution)/shard_map/all_gather | solution.py:58
  20.5 0.7 convert_element_type.6
  21.1 0.1 fusion.21
  21.3 0.7 convert_element_type.7
  22.0 0.0 collective-permute-done.1
  22.0 0.0 collective-permute-done
  22.0 1.3 fusion.10
  23.3 0.0 copy-start.2
  23.3 5.8 %convolution_bitcast_fusion = f32[2,200]{1,0:T(2,128)S(1)} fusion(f32[200,3,2048]{2,0,1:T(8,128)} %param.19, f32[3,2048]{1,0:T(4,128)} %param.16, f32[2,2048]{1,0:T(2,128)S(1)} %fusion.18), kind=kOutput, calls=%fused_computation.6 | convolution fusion | flops 29503488 | bytes 4957760 | tf_op jit(solution)/shard_map/dot_general | solution.py:65
  29.1 129.9 %psum.7 = f32[2,200]{1,0:T(2,128)S(1)} all-reduce(f32[2,200]{1,0:T(2,128)S(1)} %convolution_bitcast_fusion), channel_id=1, replica_groups=mesh['space'=64,'inst'=4] {'space'}, use_global_device_ids=true, to_apply=%region_0.1 | all-reduce | flops 400 | bytes 3200 | tf_op jit(solution)/shard_map/psum | solution.py:72
  159.1 10.7 %all-gather = f32[4,2,200]{2,1,0:T(2,128)S(1)} all-gather(f32[1,2,200]{2,1,0:T(2,128)S(1)} %bitcast.66), channel_id=1, replica_groups=mesh['space'=64,'inst'=4] {'inst'}, dimensions={0}, use_global_device_ids=true | all-gather | bytes 8000 | tf_op jit(solution)/shard_map/all_gather | solution.py:73
  169.8 0.0 copy-done.3
  169.8 0.1 fusion.6
  169.9 0.0 copy-done
  169.9 0.2 fusion.33
  170.1 5.5 %fusion.3 = f32[2,3,2048]{2,0,1:T(2,128)} fusion(f32[2048]{0:T(1024)S(1)} %convert_element_type.7, f32[2,200]{1,0:T(2,128)S(1)} %fusion.33, f32[200,3,2048]{2,0,1:T(8,128)} %param.19), kind=kOutput, calls=%fused_computation.4 | convolution fusion | flops 29503488 | bytes 4974144 | tf_op jit(solution)/shard_map/dot_general | solution.py:77
  175.6 0.0 copy-done.2
  (4 shorter events, 0.0 us)
Async XLA Ops:
  0.6 169.3 %copy-start = (f32[200,200]{1,0:T(8,128)S(1)}, f32[200,200]{1,0:T(8,128)}, u32[]{:S(2)}) copy-start(f32[200,200]{1,0:T(8,128)} %param.21) | copy-start | bytes 480004
  0.6 169.1 %copy-start.3 = (f32[200]{0:T(256)S(1)}, f32[200]{0:T(256)}, u32[]{:S(2)}) copy-start(f32[200]{0:T(256)} %param.20) | copy-start | bytes 2404
  2.9 19.1 %collective-permute-start.1 = (f32[2,2,5,1]{3,1,2,0:T(2,128)S(1)}, f32[2,2,5,1]{3,1,2,0:T(2,128)S(1)}, u32[]{:S(2)}, u32[]{:S(2)}) collective-permute-start(f32[2,2,5,1]{3,1,2,0:T(2,128)S(1)} %get-tuple-element.7), channel_id=1, source_target_pairs={{0,4},{4,8},{8,12},{12,16},{16,20},{20,24},{24,28},{28,32},{32,36}... | collective-permute-start | bytes 248 | tf_op jit(solution)/shard_map/ppermute | solution.py:14
  4.6 17.4 %collective-permute-start = (f32[2,2,5,1]{3,1,2,0:T(2,128)S(1)}, f32[2,2,5,1]{3,1,2,0:T(2,128)S(1)}, u32[]{:S(2)}, u32[]{:S(2)}) collective-permute-start(f32[2,2,5,1]{3,1,2,0:T(2,128)S(1)} %get-tuple-element.6), channel_id=1, source_target_pairs={{4,0},{8,4},{12,8},{16,12},{20,16},{24,20},{28,24},{32,28},{36,32}... | collective-permute-start | bytes 248 | tf_op jit(solution)/shard_map/ppermute | solution.py:15
  23.3 152.3 %copy-start.2 = (f32[2,5,2048]{2,0,1:T(2,128)}, f32[2,5,2048]{2,0,1:T(2,128)S(1)}, u32[]{:S(2)}) copy-start(f32[2,5,2048]{2,0,1:T(2,128)S(1)} %fusion.10) | copy-start | bytes 245764
  170.1 5.5 %copy-start.1 = (f32[2,200]{1,0:T(2,128)}, f32[2,200]{1,0:T(2,128)S(1)}, u32[]{:S(2)}) copy-start(f32[2,200]{1,0:T(2,128)S(1)} %fusion.33) | copy-start | bytes 4804
where the time goes:
time: 176 us
  blocking collectives  154 us (88%)
  matrix products  12.8 us (7%)
  other arithmetic  3.69 us (2%)
  starting transfers between devices  3.02 us (2%)
    psum x1, blocking collectives, shards(): summed = lax.psum(projected, 'space')  130 us
    all_gather x1, blocking collectives, shards(): lax.all_gather(adjoint, 'inst', axis=0, tiled=True)  13.6 us
    all_gather x1, blocking collectives, shards(): gathered = lax.all_gather(summed, 'inst', axis=0, tiled=True)  10.7 us
    dot_general x1, matrix products, shards(): lax.dot_general(force.reshape(own_slots, -1), shapes, (((1,), (1,)), ((),...  5.76 us
    dot_general x1, matrix products, shards(): jnp.dot(modal_adjoint, shapes, precision=highest).reshape(own_slots, 3, -1)  5.45 us
  transfers between devices with their start and end apart: 2, of which 0 were waited for; matrix products, arithmetic and copies ran while one was open for 1% of the time, Pallas kernels for 0%

commit v1 on v0

--- a/solution.py
+++ b/solution.py
@@ -69,7 +69,8 @@
         precision=highest,
         preferred_element_type=jnp.float32,
     )
-    summed = lax.psum(projected, "space")
+    pieces = lax.all_gather(projected, "space", axis=0, tiled=False)
+    summed = pieces.sum(axis=0)
     gathered = lax.all_gather(summed, "inst", axis=0, tiled=True)
     own_projected = lax.dynamic_slice_in_dim(gathered, first_slot, own_slots, 0)
     modal_rhs = own_projected + damping[None, :] * jnp.dot(own_cols.T, gathered, precision=highest)

time: 176 us -> 102 us (0.58)
  blocking collectives: 154 us -> 80.6 us
    psum x1 -> x0, blocking collectives: 130 us -> none  [shards(): summed = lax.psum(projected, 'space')]
    all_gather x0 -> x1, blocking collectives: none -> 56.2 us  [shards(): pieces = lax.all_gather(projected, 'space', axis=0, tiled=False)]
  transfers between devices with their start and end apart: 2 -> 2, of which waited for: 0 -> 0; matrix products, arithmetic and copies ran while one was open for 1% -> 2% of each run, Pallas kernels for 0% -> 0%
where the time goes in v1:
time: 102 us
  blocking collectives  80.6 us (79%)
  matrix products  12.8 us (13%)
  other arithmetic  3.78 us (4%)
  starting transfers between devices  3.02 us (3%)
    all_gather x1, blocking collectives, shards(): pieces = lax.all_gather(projected, 'space', axis=0, tiled=False)  56.2 us
    all_gather x1, blocking collectives, shards(): lax.all_gather(adjoint, 'inst', axis=0, tiled=True)  13.6 us
    all_gather x1, blocking collectives, shards(): gathered = lax.all_gather(summed, 'inst', axis=0, tiled=True)  10.7 us
    dot_general x1, matrix products, shards(): lax.dot_general(force.reshape(own_slots, -1), shapes, (((1,), (1,)), ((),...  5.76 us
    dot_general x1, matrix products, shards(): jnp.dot(modal_adjoint, shapes, precision=highest).reshape(own_slots, 3, -1)  5.45 us
    dot_general x1, other arithmetic, shards(): flow = jnp.einsum('sfec,sfc->sec', jac_cell, adjoint, precision=highest)  2.12 us
  transfers between devices with their start and end apart: 2, of which 0 were waited for; matrix products, arithmetic and copies ran while one was open for 2% of the time, Pallas kernels for 0%

profile of v1, /device:TPU:8, one launch (start us, length us, event | category | flops | bytes accessed | tf_op | source)
XLA Modules:
  0.0 101.9 jit_solution(11380316839315550119)
XLA Ops:
  0.6 0.0 copy-start
  0.6 0.0 copy-start.3
  0.7 2.1 %multiply_reduce_fusion.2 = (f32[2,2048,5]{1,0,2:T(2,128)S(1)}, f32[2,2048,5]{1,0,2:T(2,128)S(1)}, f32[2,2048,5]{1,0,2:T(2,128)S(1)}) fusion(f32[2,5,5,2048]{3,0,2,1:T(2,128)} %param.12, f32[2,2048,5]{1,0,2:T(2,128)} %bitcast.62, f32[2,5,5,2048]{3,0,2,1:T(2,128)} %param.13, f32[2,5,5,2048]{3,0,2,1:T(2,128)} %param.14), kind=kLoop, calls=%fused_computation.10 | loop fusion | flops 552960 | bytes 1556480 | tf_op jit(solution)/shard_map/sfec,sfc->sec/dot_general | solution.py:49
  2.8 0.1 pad_maximum_fusion.5
  2.9 1.7 %collective-permute-start.1 = (f32[2,2,5,1]{3,1,2,0:T(2,128)S(1)}, f32[2,2,5,1]{3,1,2,0:T(2,128)S(1)}, u32[]{:S(2)}, u32[]{:S(2)}) collective-permute-start(f32[2,2,5,1]{3,1,2,0:T(2,128)S(1)} %get-tuple-element.7), channel_id=1, source_target_pairs={{0,4},{4,8},{8,12},{12,16},{16,20},{20,24},{24,28},{28,32},{32,36}... | collective-permute-start | bytes 248 | tf_op jit(solution)/shard_map/ppermute | solution.py:14
  4.6 1.3 %collective-permute-start = (f32[2,2,5,1]{3,1,2,0:T(2,128)S(1)}, f32[2,2,5,1]{3,1,2,0:T(2,128)S(1)}, u32[]{:S(2)}, u32[]{:S(2)}) collective-permute-start(f32[2,2,5,1]{3,1,2,0:T(2,128)S(1)} %get-tuple-element.6), channel_id=1, source_target_pairs={{4,0},{8,4},{12,8},{16,12},{20,16},{24,20},{28,24},{32,28},{36,32}... | collective-permute-start | bytes 248 | tf_op jit(solution)/shard_map/ppermute | solution.py:15
  5.9 0.9 copy.16
  6.8 13.6 %all_gather.12 = f32[8,5,2048]{2,1,0:T(8,128)S(1)} all-gather(f32[2,5,2048]{2,1,0:T(8,128)S(1)} %copy.16), channel_id=1, replica_groups=mesh['space'=64,'inst'=4] {'inst'}, dimensions={0}, use_global_device_ids=true | all-gather | bytes 409600 | tf_op jit(solution)/shard_map/all_gather | solution.py:58
  20.5 0.7 convert_element_type.6
  21.1 0.1 fusion.21
  21.3 0.7 convert_element_type.7
  22.0 0.0 collective-permute-done.1
  22.0 0.0 collective-permute-done
  22.0 1.3 %fusion.10 = f32[2,5,2048]{2,0,1:T(2,128)S(1)} fusion(f32[2,2,5,1]{3,1,2,0:T(2,128)S(1)} %collective-permute-done.1, f32[1,2,5,2048]{3,1,2,0:T(2,128)S(1)} %bitcast.66, f32[1,2,5,2048]{3,1,2,0:T(2,128)S(1)} %bitcast.64, f32[2,2,5,1]{3,1,2,0:T(2,128)S(1)} %collective-permute-done, f32[2,2048,5]{1,0,2:T(2,128)S(1)} %get-tuple-element.3, ...), kind=kOutput, calls=%fused_computation.15 | convolution fusion | flops 2129920 | bytes 881668 | tf_op jit(solution)/shard_map/ab,aec->bec/dot_general | solution.py:55
  23.3 0.0 copy-start.2
  23.3 5.8 %convolution_bitcast_fusion = f32[1,2,200]{2,1,0:T(2,128)S(1)} fusion(f32[200,3,2048]{2,0,1:T(8,128)} %param.19, f32[3,2048]{1,0:T(4,128)} %param.16, f32[2,2048]{1,0:T(2,128)S(1)} %fusion.18), kind=kOutput, calls=%fused_computation.6 | convolution fusion | flops 29503488 | bytes 4957760 | tf_op jit(solution)/shard_map/dot_general | solution.py:65
  29.1 56.2 %all-gather.1 = f32[64,2,200]{2,1,0:T(2,128)S(1)} all-gather(f32[1,2,200]{2,1,0:T(2,128)S(1)} %convolution_bitcast_fusion), channel_id=2, replica_groups=mesh['space'=64,'inst'=4] {'space'}, dimensions={0}, use_global_device_ids=true | all-gather | bytes 104000 | tf_op jit(solution)/shard_map/all_gather | solution.py:72
  85.3 0.1 reduce_sum.9
  85.4 10.7 %all-gather.2 = f32[4,2,200]{2,1,0:T(2,128)S(1)} all-gather(f32[1,2,200]{2,1,0:T(2,128)S(1)} %bitcast.67), channel_id=1, replica_groups=mesh['space'=64,'inst'=4] {'inst'}, dimensions={0}, use_global_device_ids=true | all-gather | bytes 8000 | tf_op jit(solution)/shard_map/all_gather | solution.py:74
  96.2 0.0 copy-done.3
  96.2 0.1 fusion.6
  96.3 0.0 copy-done
  96.3 0.2 fusion.33
  96.5 5.5 %fusion.3 = f32[2,3,2048]{2,0,1:T(2,128)} fusion(f32[2048]{0:T(1024)S(1)} %convert_element_type.7, f32[2,200]{1,0:T(2,128)S(1)} %fusion.33, f32[200,3,2048]{2,0,1:T(8,128)} %param.19), kind=kOutput, calls=%fused_computation.4 | convolution fusion | flops 29503488 | bytes 4974144 | tf_op jit(solution)/shard_map/dot_general | solution.py:78
  (5 shorter events, 0.0 us)
Async XLA Ops:
  0.6 95.7 %copy-start = (f32[200,200]{1,0:T(8,128)S(1)}, f32[200,200]{1,0:T(8,128)}, u32[]{:S(2)}) copy-start(f32[200,200]{1,0:T(8,128)} %param.21) | copy-start | bytes 480004
  0.6 95.5 %copy-start.3 = (f32[200]{0:T(256)S(1)}, f32[200]{0:T(256)}, u32[]{:S(2)}) copy-start(f32[200]{0:T(256)} %param.20) | copy-start | bytes 2404
  2.9 19.1 %collective-permute-start.1 = (f32[2,2,5,1]{3,1,2,0:T(2,128)S(1)}, f32[2,2,5,1]{3,1,2,0:T(2,128)S(1)}, u32[]{:S(2)}, u32[]{:S(2)}) collective-permute-start(f32[2,2,5,1]{3,1,2,0:T(2,128)S(1)} %get-tuple-element.7), channel_id=1, source_target_pairs={{0,4},{4,8},{8,12},{12,16},{16,20},{20,24},{24,28},{28,32},{32,36}... | collective-permute-start | bytes 248 | tf_op jit(solution)/shard_map/ppermute | solution.py:14
  4.6 17.4 %collective-permute-start = (f32[2,2,5,1]{3,1,2,0:T(2,128)S(1)}, f32[2,2,5,1]{3,1,2,0:T(2,128)S(1)}, u32[]{:S(2)}, u32[]{:S(2)}) collective-permute-start(f32[2,2,5,1]{3,1,2,0:T(2,128)S(1)} %get-tuple-element.6), channel_id=1, source_target_pairs={{4,0},{8,4},{12,8},{16,12},{20,16},{24,20},{28,24},{32,28},{36,32}... | collective-permute-start | bytes 248 | tf_op jit(solution)/shard_map/ppermute | solution.py:15
  23.3 78.6 %copy-start.2 = (f32[2,5,2048]{2,0,1:T(2,128)}, f32[2,5,2048]{2,0,1:T(2,128)S(1)}, u32[]{:S(2)}) copy-start(f32[2,5,2048]{2,0,1:T(2,128)S(1)} %fusion.10) | copy-start | bytes 245764
  96.5 5.5 %copy-start.1 = (f32[2,200]{1,0:T(2,128)}, f32[2,200]{1,0:T(2,128)S(1)}, u32[]{:S(2)}) copy-start(f32[2,200]{1,0:T(2,128)S(1)} %fusion.33) | copy-start | bytes 4804
